TPU v7x, 1024 devices: a whole 4x8x16 slice. The times are simulated.
1024 devices in a mesh: section: 16 (over z), expert: 64 (over x, y, core).
Axes of the slice: x: 4, y: 8, z: 16, core: 2. Of those that a mesh axis runs over, the one named last changes fastest.
Arguments:
- route_ids: int32 [1, 131072, 1], P(None, ('section', 'expert')), may hold values from 0 to 7; in each aligned block of 128 rows (0 to 127, 128 to 255, ..., all dimensions but the last counted through in order) at most 18 rows name the same one
- gate_pre: bfloat16 [16, 1, 64, 1152, 128], P('section', None, 'expert'), may hold values from -6 to 6
- up_pre: bfloat16 [16, 1, 64, 1152, 128], P('section', None, 'expert'), may hold values from -6 to 6
- hid_grad: bfloat16 [16, 1, 64, 1152, 128], P('section', None, 'expert'), may hold values from -6 to 6
- w_gate: bfloat16 [16, 64, 448, 1024], P('section', 'expert'), may hold values from -0.1875 to 0.1875
- w_up: bfloat16 [16, 64, 448, 1024], P('section', 'expert'), may hold values from -0.1875 to 0.1875
Outputs:
- to_previous: bfloat16 [1, 131072, 3584], P(None, ('section', 'expert'))
Inputs may be any that keep to these rules, and one draw needn't show every extreme that they name: `route_ids`: in each micro-batch, no expert is named by more than 18 routes of one device's tokens, a bound that some block reaches of them; a token's routes name different experts.
All inputs are finite; a program needn't handle non-finite values.
Results may differ from a plain program's by a relative error of at most 0.0049.
Values may be sent and summed in bfloat16 or wider, within the bound.
A program may use at most 32 MiB of HBM per device.

v0:
```python
import jax
import jax.numpy as jnp
from jax import lax
from jax.sharding import PartitionSpec as P

GRP = 8


def partner_2(x, axis, apart):
    return lax.ppermute(x, axis, [(i, i ^ 1 << apart) for i in range(lax.axis_size(axis))])


def shifted(value, axis, steps):
    count = lax.axis_size(axis)
    leading, last = (max(0, -steps), min(count, count - steps))
    return lax.ppermute(value, axis, [(source, source + steps) for source in range(leading, last)])


def derivatives(gate_part, up_part, grad_part):
    gate_val = gate_part.astype(jnp.float32)
    up_val = up_part.astype(jnp.float32)
    grad_val = grad_part.astype(jnp.float32)
    sigma = jax.nn.sigmoid(gate_val)
    gate_grad = (grad_val * up_val * sigma * (1.0 + gate_val * (1.0 - sigma))).astype(jnp.bfloat16)
    up_grad = (grad_val * gate_val * sigma).astype(jnp.bfloat16)
    return (gate_grad, up_grad)


def collect_group(pieces, position):
    levels = GRP.bit_length() - 1
    order = list(range(levels))
    for level in order:
        partner = partner_2(pieces, "expert", level)
        lower = position // 2**level % 2 == 0
        pieces = jnp.where(
            lower, jnp.concatenate([pieces, partner], 1), jnp.concatenate([partner, pieces], 1)
        )
    return pieces


def slot_rows(pieces, gate_weight, up_weight):
    feat_count = gate_weight.shape[0]
    gate_split = gate_weight.reshape(feat_count, GRP, -1)
    up_split = up_weight.reshape(feat_count, GRP, -1)
    summed = jnp.einsum("qsh,dqh->sd", pieces[0], gate_split, preferred_element_type=jnp.float32)
    summed = summed + jnp.einsum(
        "qsh,dqh->sd", pieces[1], up_split, preferred_element_type=jnp.float32
    )
    return summed.astype(jnp.bfloat16)


def token_rows(received, routes, capacity):
    expert_count = received.shape[0] // (GRP * capacity)
    tok_count = routes.shape[0]
    flat = routes.reshape(-1)
    onehot = (flat[:, None] == jnp.arange(expert_count, dtype=jnp.int32)[None, :]).astype(jnp.int32)
    earlier = jnp.cumsum(onehot, axis=0) - onehot
    slot_pos = jnp.sum(onehot * earlier, axis=1)
    blocks = received.reshape(expert_count, GRP, capacity, received.shape[1])
    picked = blocks[flat, :, slot_pos, :]
    widened = picked.reshape(tok_count, routes.shape[1], -1).astype(jnp.float32)
    return jnp.sum(widened, axis=1).astype(jnp.bfloat16)


def local(route_ids, gate_pre, up_pre, hid_grad, w_gate, w_up):
    position = lax.axis_index("expert")
    devices = lax.axis_size("expert")
    capacity = gate_pre.shape[3] // devices
    gate_grad, up_grad = derivatives(gate_pre[0, 0, 0], up_pre[0, 0, 0], hid_grad[0, 0, 0])
    pieces = collect_group(jnp.stack([gate_grad, up_grad])[:, None], position)
    rows_out = slot_rows(pieces, w_gate[0, 0], w_up[0, 0])
    received = lax.all_to_all(rows_out[None], "expert", split_axis=1, concat_axis=1, tiled=True)
    results = [token_rows(received[0], route_ids[0], capacity)]
    grads = jnp.stack(results)
    return shifted(grads, "section", -1)


def solution(mesh):
    placed = (
        P(None, ("section", "expert"), None),
        P("section", None, "expert", None, None),
        P("section", None, "expert", None, None),
        P("section", None, "expert", None, None),
        P("section", "expert", None, None),
        P("section", "expert", None, None),
    )
    return jax.shard_map(
        local,
        mesh=mesh,
        in_specs=placed,
        out_specs=P(None, ("section", "expert"), None),
        check_vma=False,
    )
```

profile of v0, /device:TPU:1, one launch (start us, length us, event | category | flops | bytes accessed | tf_op | source)
XLA Modules:
  0.0 248.7 jit_solution(4294528364152455098)
XLA Ops:
  0.0 1.5 fusion.7
  1.5 0.1 maximum_bitcast_fusion
  1.5 16.0 %collective-permute-start = (bf16[2,1,1152,128]{3,2,1,0:T(8,128)(2,1)S(1)}, bf16[2,1,1152,128]{3,2,1,0:T(8,128)(2,1)S(1)}, u32[]{:S(2)}, u32[]{:S(2)}) collective-permute-start(bf16[2,1,1152,128]{3,2,1,0:T(8,128)(2,1)S(1)} %maximum_bitcast_fusion), channel_id=1, source_target_pairs={{0,1},{1,0},{2,3},{3,2},{4,5},{5,4},{6,7},{7,6},{8,9},{9,8},{10,11... | collective-permute-start | bytes 1769480 | tf_op jit(solution)/shard_map/ppermute | solution.py:10
  17.6 1.6 collective-permute-done
  19.2 0.2 maximum_select_fusion.2
  19.4 1.9 collective-permute-start.1
  21.3 27.2 %collective-permute-done.1 = bf16[2,2,1152,128]{3,2,1,0:T(8,128)(2,1)} collective-permute-done((bf16[2,2,1152,128]{3,2,1,0:T(8,128)(2,1)S(1)}, bf16[2,2,1152,128]{3,2,1,0:T(8,128)(2,1)}, u32[]{:S(2)}, u32[]{:S(2)}) %collective-permute-start.1) | collective-permute-done | bytes 1179680 | tf_op jit(solution)/shard_map/ppermute | solution.py:10
  48.5 1.9 maximum_select_fusion.1
  50.4 1.9 collective-permute-start.2
  52.3 1.4 copy.24
  53.7 1.4 copy.23
  55.2 101.8 %collective-permute-done.2 = bf16[2,4,1152,128]{3,2,1,0:T(8,128)(2,1)} collective-permute-done((bf16[2,4,1152,128]{3,2,1,0:T(8,128)(2,1)S(1)}, bf16[2,4,1152,128]{3,2,1,0:T(8,128)(2,1)}, u32[]{:S(2)}, u32[]{:S(2)}) %collective-permute-start.2) | collective-permute-done | bytes 2359328 | tf_op jit(solution)/shard_map/ppermute | solution.py:10
  157.0 3.3 %maximum_select_fusion = bf16[2,8,1152,128]{3,2,1,0:T(8,128)(2,1)S(1)} fusion(bf16[2,4,1152,128]{3,2,1,0:T(8,128)(2,1)} %collective-permute-done.2, bf16[2,4,1152,128]{3,2,1,0:T(8,128)(2,1)S(1)} %maximum_select_fusion.1, pred[]{:T(512)S(6)} %eq.28), kind=kLoop, calls=%fused_computation.1 | loop fusion | flops 7077888 | bytes 9437185 | tf_op jit(solution)/shard_map/jit(_where)/select_n | solution.py:35
  160.3 1.4 convolution_bitcast_fusion
  161.7 1.4 fusion.2
  163.1 5.8 %copy.18 = bf16[1,1152,448]{2,0,1:T(2,128)(2,1)S(1)} copy(bf16[1,1152,448]{1,2,0:T(8,128)(2,1)S(1)} %fusion.2) | data formatting | bytes 2064384 | tf_op jit(solution)/shard_map/broadcast_in_dim | solution.py:72
  168.9 0.5 broadcast.103
  169.4 7.6 %reduce.2 = bf16[1152,448]{1,0:T(8,128)(2,1)S(1)} reduce(bf16[1152,1,448]{2,1,0:T(2,128)(2,1)S(1)} %bitcast.54, bf16[]{:T(256)} %broadcast.103), dimensions={1}, to_apply=%bitcast.51.reduce_sub_computation | reduce | bytes 2064386
  177.1 0.0 copy-start
  177.1 2.2 reshape.150
  179.3 4.6 %all-to-all-start = ((bf16[64,2,4032]{2,1,0:T(2,128)(2,1)}), bf16[64,2,4032]{2,1,0:T(2,128)(2,1)S(1)}, u32[]{:S(2)}, u32[]{:S(2)}) async-start(bf16[64,2,4032]{2,1,0:T(2,128)(2,1)} %reshape.150), calls=%async_computation | async-start | bytes 2097152 | tf_op jit(solution)/shard_map/all_to_all | solution.py:72
  183.9 0.0 copy-done
  183.9 0.1 fusion.14
  184.0 0.2 reduce_window_sum.11
  184.1 0.2 select_reduce_fusion
  184.3 28.1 %all-to-all-done = bf16[64,2,4032]{2,1,0:T(2,128)(2,1)S(1)} async-done(((bf16[64,2,4032]{2,1,0:T(2,128)(2,1)}), bf16[64,2,4032]{2,1,0:T(2,128)(2,1)S(1)}, u32[]{:S(2)}, u32[]{:S(2)}) %all-to-all-start) | async-done | bytes 1032224 | tf_op jit(solution)/shard_map/all_to_all | solution.py:72
  212.4 1.5 reshape.151
  214.0 7.0 %bitcast_reduce_fusion = bf16[1152,448]{1,0:T(8,128)(2,1)S(1)} fusion(bf16[1152,1,448]{2,1,0:T(2,128)(2,1)S(1)} %reshape.151), kind=kLoop, calls=%fused_computation.38 | loop fusion | bytes 2064384 | tf_op jit(solution)/shard_map/all_to_all | solution.py:72
  220.9 0.5 reshape_squeeze.14
  221.4 0.4 copy.19
  221.8 0.9 gather_fusion
  222.7 1.1 copy.20
  223.8 1.3 collective-permute-start.3
  225.1 22.3 %collective-permute-done.3 = bf16[1,128,3584]{1,2,0:T(8,128)(2,1)S(1)} collective-permute-done((bf16[1,128,3584]{1,2,0:T(8,128)(2,1)S(1)}, bf16[1,128,3584]{1,2,0:T(8,128)(2,1)S(1)}, u32[]{:S(2)}, u32[]{:S(2)}) %collective-permute-start.3) | collective-permute-done | bytes 917536 | tf_op jit(solution)/shard_map/ppermute | solution.py:16
  247.5 1.3 copy.21
  (1 shorter events, 0.0 us)
Async XLA Ops:
  1.5 17.6 %collective-permute-start = (bf16[2,1,1152,128]{3,2,1,0:T(8,128)(2,1)S(1)}, bf16[2,1,1152,128]{3,2,1,0:T(8,128)(2,1)S(1)}, u32[]{:S(2)}, u32[]{:S(2)}) collective-permute-start(bf16[2,1,1152,128]{3,2,1,0:T(8,128)(2,1)S(1)} %maximum_bitcast_fusion), channel_id=1, source_target_pairs={{0,1},{1,0},{2,3},{3,2},{4,5},{5,4},{6,7},{7,6},{8,9},{9,8},{10,11... | collective-permute-start | bytes 1769480 | tf_op jit(solution)/shard_map/ppermute | solution.py:10
  19.4 29.2 %collective-permute-start.1 = (bf16[2,2,1152,128]{3,2,1,0:T(8,128)(2,1)S(1)}, bf16[2,2,1152,128]{3,2,1,0:T(8,128)(2,1)}, u32[]{:S(2)}, u32[]{:S(2)}) collective-permute-start(bf16[2,2,1152,128]{3,2,1,0:T(8,128)(2,1)S(1)} %maximum_select_fusion.2), channel_id=1, source_target_pairs={{0,2},{1,3},{2,0},{3,1},{4,6},{5,7},{6,4},{7,5},{8,10},{9,11},{10,... | collective-permute-start | bytes 3538952 | tf_op jit(solution)/shard_map/ppermute | solution.py:10
  50.4 106.6 %collective-permute-start.2 = (bf16[2,4,1152,128]{3,2,1,0:T(8,128)(2,1)S(1)}, bf16[2,4,1152,128]{3,2,1,0:T(8,128)(2,1)}, u32[]{:S(2)}, u32[]{:S(2)}) collective-permute-start(bf16[2,4,1152,128]{3,2,1,0:T(8,128)(2,1)S(1)} %maximum_select_fusion.1), channel_id=1, source_target_pairs={{0,4},{1,5},{2,6},{3,7},{4,0},{5,1},{6,2},{7,3},{8,12},{9,13},{10,... | collective-permute-start | bytes 7077896 | tf_op jit(solution)/shard_map/ppermute | solution.py:10
  177.1 6.8 %copy-start = (s32[1,128,1]{1,2,0:T(1,128)S(1)}, s32[1,128,1]{1,2,0:T(1,128)}, u32[]{:S(2)}) copy-start(s32[1,128,1]{1,2,0:T(1,128)} %param.6) | copy-start | bytes 1540
  179.3 33.1 %all-to-all-start = ((bf16[64,2,4032]{2,1,0:T(2,128)(2,1)}), bf16[64,2,4032]{2,1,0:T(2,128)(2,1)S(1)}, u32[]{:S(2)}, u32[]{:S(2)}) async-start(bf16[64,2,4032]{2,1,0:T(2,128)(2,1)} %reshape.150), calls=%async_computation | async-start | bytes 2097152 | tf_op jit(solution)/shard_map/all_to_all | solution.py:72
  223.8 23.6 %collective-permute-start.3 = (bf16[1,128,3584]{1,2,0:T(8,128)(2,1)S(1)}, bf16[1,128,3584]{1,2,0:T(8,128)(2,1)S(1)}, u32[]{:S(2)}, u32[]{:S(2)}) collective-permute-start(bf16[1,128,3584]{1,2,0:T(8,128)(2,1)S(1)} %bitcast.59), channel_id=1, source_target_pairs={{64,0},{128,64},{192,128},{256,192},{320,256},{384,320},{448,384},... | collective-permute-start | bytes 2752520 | tf_op jit(solution)/shard_map/ppermute | solution.py:16
where the time goes:
time: 249 us
  waiting for transfers between devices  181 us (73%)
  starting transfers between devices  25.7 us (10%)
  local copies, waits for them, and re-layouts  23.9 us (10%)
  other arithmetic  14.9 us (6%)
  matrix products  2.8 us (1%)
    ppermute x3, waiting for transfers between devices, partner_2(): lax.ppermute(x, axis, [(i, i ^ 1 << apart) for i in range(lax.axis_size(a...  131 us
    all_to_all x1, waiting for transfers between devices, local(): lax.all_to_all(rows_out[None], 'expert', split_axis=1, concat_axis=1, til...  28.1 us
    ppermute x1, waiting for transfers between devices, shifted(): lax.ppermute(value, axis, [(source, source + steps) for source in range(l...  22.3 us
    ppermute x3, starting transfers between devices, partner_2(): lax.ppermute(x, axis, [(i, i ^ 1 << apart) for i in range(lax.axis_size(a...  19.9 us
    unnamed x1, other arithmetic  7.64 us
    unnamed x7, local copies, waits for them, and re-layouts  7.04 us
    all_to_all x1, local copies, waits for them, and re-layouts, local(): lax.all_to_all(rows_out[None], 'expert', split_axis=1, concat_axis=1, til...  6.98 us
    broadcast_in_dim x1, local copies, waits for them, and re-layouts, local(): rows_out[None]  5.78 us
  transfers between devices with their start and end apart: 5, of which 5 were waited for; matrix products, arithmetic and copies ran while one was open for 1% of the time, Pallas kernels for 0%

commit v1 on v0

v1 whole, which is shorter than its diff:
```python
import functools

import jax
import jax.numpy as jnp
from jax import lax
from jax.experimental import pallas as pl
from jax.experimental.pallas import tpu as pltpu
from jax.sharding import PartitionSpec as P

GRP = 8
CHIPS = 4
ROUNDS = 4
LANES = 128
MESH = pl.DeviceIdType.MESH


def kernel(
    sections, devices, cap,
    ids_ref, gate_ref, up_ref, hid_ref, wg_ref, wu_ref,
    out_ref,
    act, other, weight, acc, stage, msg, recv, ids_in, pick,
    act_recv, own_send, fwd_send, w_send, w_recv, w_local, id_send, id_recv, msg_send, msg_recv,
):
    experts = devices // GRP
    half = devices // 2
    per_round = half // ROUNDS
    rows = per_round * cap
    half_rows = half * cap
    feats = wg_ref.shape[0]
    blocks = 2 * feats // LANES

    s = lax.axis_index("section")
    p = lax.axis_index("expert")
    e = p // GRP
    c = (p % GRP) // 2
    k = p % 2
    turn = e % ROUNDS

    def near(chip, core):
        return (s, e * GRP + chip * 2 + core)

    has_left, has_right = c > 0, c < CHIPS - 1
    sends_back, gets_back = s > 0, s < sections - 1

    barrier = pltpu.get_barrier_semaphore()

    def greet(device):
        pl.semaphore_signal(barrier, inc=1, device_id=device, device_id_type=MESH)

    greet(near(c, 1 - k))

    @pl.when(has_left)
    def _():
        greet(near(c - 1, 0))
        greet(near(c - 1, 1))

    @pl.when(has_right)
    def _():
        greet(near(c + 1, 0))
        greet(near(c + 1, 1))

    @pl.when(gets_back)
    def _():
        greet((s + 1, p))
        owner_half = p // half

        def step(i, carry):
            greet((s + 1, 2 * i + owner_half))
            return carry

        lax.fori_loop(0, devices // 2, step, 0)

    w_rows = pl.ds(pl.multiple_of(k * feats, feats), feats)
    local_g = pltpu.make_async_copy(wg_ref, weight.at[0, w_rows], w_local.at[0])
    local_u = pltpu.make_async_copy(wu_ref, weight.at[1, w_rows], w_local.at[1])
    local_g.start()
    local_u.start()

    def derive(start):
        at = pl.ds(pl.multiple_of(start, 16), rows)
        gate_val = gate_ref[at, :].astype(jnp.float32)
        up_val = up_ref[at, :].astype(jnp.float32)
        grad_val = hid_ref[at, :].astype(jnp.float32)
        sigma = jax.nn.sigmoid(gate_val)
        part = grad_val * sigma
        gate_grad = part * up_val * (1.0 + gate_val * (1.0 - sigma))
        return gate_grad.astype(jnp.bfloat16), (part * gate_val).astype(jnp.bfloat16)

    def derive_round(r, carry):
        chunk = (r + turn) % ROUNDS
        gate_grad, up_grad = derive(k * half_rows + chunk * rows)
        act[c, r, k, :, :LANES] = gate_grad
        act[c, r, k, :, LANES:] = up_grad
        gate_grad, up_grad = derive((1 - k) * half_rows + chunk * rows)
        other[r, :, :LANES] = gate_grad
        other[r, :, LANES:] = up_grad
        return carry

    lax.fori_loop(0, ROUNDS, derive_round, 0)

    pl.semaphore_wait(
        barrier,
        1
        + 2 * has_left.astype(jnp.int32)
        + 2 * has_right.astype(jnp.int32)
        + (devices // 2 + 1) * sends_back.astype(jnp.int32),
    )

    def remote(src, dst, send, recv_sem, device):
        return pltpu.make_async_remote_copy(
            src_ref=src, dst_ref=dst, send_sem=send, recv_sem=recv_sem,
            device_id=device, device_id_type=MESH,
        )

    def own_copies(r, chip, side):
        same = remote(
            act.at[c, r, k], act.at[c, r, k], own_send.at[r, 2 * side], act_recv.at[c, r, k], near(chip, k)
        )
        cross = remote(
            other.at[r], act.at[c, r, k], own_send.at[r, 2 * side + 1], act_recv.at[c, r, k], near(chip, 1 - k)
        )
        return same, cross

    def own_partner(r):
        return remote(
            other.at[r], act.at[c, r, k], own_send.at[r, 4], act_recv.at[c, r, k], near(c, 1 - k)
        )

    def forward(r, source, chip, slot):
        return remote(
            act.at[source, r], act.at[source, r], fwd_send.at[r, slot], act_recv.at[source, r, 0], near(chip, k)
        )

    def each_own(r, what):
        @pl.when(has_left)
        def _():
            for copy in own_copies(r, c - 1, 0):
                what(copy)

        @pl.when(has_right)
        def _():
            for copy in own_copies(r, c + 1, 1):
                what(copy)

        what(own_partner(r))

    def arrived(ref, sem):
        pltpu.make_async_copy(ref, ref, sem).wait()

    weight_g = remote(wg_ref, weight.at[0, w_rows], w_send.at[0], w_recv.at[0], near(c, 1 - k))
    weight_u = remote(wu_ref, weight.at[1, w_rows], w_send.at[1], w_recv.at[1], near(c, 1 - k))
    id_copy = remote(ids_ref, ids_in, id_send.at[0], id_recv.at[0], (s - 1, p))

    each_own(0, lambda copy: copy.start())
    weight_g.start()
    weight_u.start()

    @pl.when(sends_back)
    def _():
        id_copy.start()

    stage[...] = jnp.zeros_like(stage)

    def back(r, i):
        owner = k * half + ((r + turn) % ROUNDS) * per_round + i
        return remote(
            msg.at[r, i], recv.at[c, e], msg_send.at[r, i], msg_recv.at[c, e], (s - 1, owner)
        )

    def round_step(r, carry):
        @pl.when(r + 1 < ROUNDS)
        def _():
            each_own(r + 1, lambda copy: copy.start())

        @pl.when(has_left)
        def _():
            arrived(act.at[c - 1, r, 0], act_recv.at[c - 1, r, 0])
            arrived(act.at[c - 1, r, 1], act_recv.at[c - 1, r, 1])

            @pl.when(has_right)
            def _():
                forward(r, c - 1, c + 1, 0).start()

        @pl.when(has_right)
        def _():
            arrived(act.at[c + 1, r, 0], act_recv.at[c + 1, r, 0])
            arrived(act.at[c + 1, r, 1], act_recv.at[c + 1, r, 1])

            @pl.when(has_left)
            def _():
                forward(r, c + 1, c - 1, 1).start()

        @pl.when(c >= 2)
        def _():
            arrived(act.at[c - 2, r], act_recv.at[c - 2, r, 0])

            @pl.when(has_right)
            def _():
                forward(r, c - 2, c + 1, 2).start()

        @pl.when(c < CHIPS - 2)
        def _():
            arrived(act.at[c + 2, r], act_recv.at[c + 2, r, 0])

            @pl.when(has_left)
            def _():
                forward(r, c + 2, c - 1, 3).start()

        arrived(act.at[c, r, 1 - k], act_recv.at[c, r, 1 - k])

        @pl.when(r == 0)
        def _():
            local_g.wait()
            local_u.wait()
            partner_rows = pl.ds(pl.multiple_of((1 - k) * feats, feats), feats)
            arrived(weight.at[0, partner_rows], w_recv.at[0])
            arrived(weight.at[1, partner_rows], w_recv.at[1])

        @pl.when(c == CHIPS - 1)
        def _():
            arrived(act.at[0, r], act_recv.at[0, r, 0])

        @pl.when(c == 0)
        def _():
            arrived(act.at[CHIPS - 1, r], act_recv.at[CHIPS - 1, r, 0])

        lhs = [
            jnp.concatenate(
                [act[chip, r, core, :, g * LANES:(g + 1) * LANES] for chip in range(CHIPS) for core in range(2)],
                axis=1,
            )
            for g in range(2)
        ]
        contract = (((1,), (1,)), ((), ()))
        for start in range(0, 2 * feats, 2 * LANES):
            size = min(2 * LANES, 2 * feats - start)
            total = None
            for g in range(2):
                term = lax.dot_general(
                    lhs[g], weight[g, start:start + size, :], contract, preferred_element_type=jnp.float32
                )
                total = term if total is None else total + term
            acc[:, start:start + size] = total

        for i in range(per_round):
            for n in range(blocks):
                stage[i % 2, n * cap:(n + 1) * cap, :] = acc[i * cap:(i + 1) * cap, n * LANES:(n + 1) * LANES]
            msg[r, i] = stage[i % 2].astype(jnp.bfloat16)

        @pl.when(sends_back)
        def _():
            def send(i, carry):
                back(r, (i + 2 * c + e) % per_round).start()
                return carry

            lax.fori_loop(0, per_round, send, 0)

        return carry

    lax.fori_loop(0, ROUNDS, round_step, 0)

    deep = recv.shape[2]
    width = experts * deep
    tokens = ids_ref.shape[1]

    @pl.when(gets_back)
    def _():
        arrived(ids_in, id_recv.at[0])
        row = jnp.broadcast_to(ids_in[...], (tokens, tokens))
        ti = lax.broadcasted_iota(jnp.int32, (tokens, tokens), 0)
        tj = lax.broadcasted_iota(jnp.int32, (tokens, tokens), 1)
        expert = jnp.sum(jnp.where(ti == tj, row, 0), axis=1, keepdims=True)
        earlier = jnp.where((row == expert) & (tj < ti), 1, 0)
        place = jnp.sum(earlier, axis=1, keepdims=True) + expert * deep
        lane = lax.broadcasted_iota(jnp.int32, (tokens, width), 1) - place
        for n in range(blocks):
            pick[n * tokens:(n + 1) * tokens, :] = jnp.where(lane == n * cap, 1.0, 0.0).astype(jnp.bfloat16)

        for chip in range(CHIPS):
            for expert_at in range(experts):
                arrived(recv.at[chip, expert_at], msg_recv.at[chip, expert_at])

        for pair in range(0, CHIPS, 2):
            rhs = jnp.concatenate(
                [recv[pair].reshape(width, LANES), recv[pair + 1].reshape(width, LANES)], axis=1
            )
            got = jnp.dot(pick[...], rhs, preferred_element_type=jnp.float32).astype(jnp.bfloat16)
            for j in range(2):
                for n in range(blocks):
                    at = ((pair + j) * blocks + n) * LANES
                    out_ref[:, at:at + LANES] = got[n * tokens:(n + 1) * tokens, j * LANES:(j + 1) * LANES]

    @pl.when(jnp.logical_not(gets_back))
    def _():
        out_ref[...] = jnp.zeros_like(out_ref)

    weight_g.wait_send()
    weight_u.wait_send()

    @pl.when(sends_back)
    def _():
        id_copy.wait_send()

    def drain(r, carry):
        each_own(r, lambda copy: copy.wait_send())

        @pl.when(has_left & has_right)
        def _():
            forward(r, c - 1, c + 1, 0).wait_send()
            forward(r, c + 1, c - 1, 1).wait_send()

        @pl.when((c >= 2) & has_right)
        def _():
            forward(r, c - 2, c + 1, 2).wait_send()

        @pl.when((c < CHIPS - 2) & has_left)
        def _():
            forward(r, c + 2, c - 1, 3).wait_send()

        @pl.when(sends_back)
        def _():
            def done(i, carry):
                back(r, i).wait_send()
                return carry

            lax.fori_loop(0, per_round, done, 0)

        return carry

    lax.fori_loop(0, ROUNDS, drain, 0)


def local(route_ids, gate_pre, up_pre, hid_grad, w_gate, w_up):
    sections, devices = lax.axis_size("section"), lax.axis_size("expert")
    slots, hidden = gate_pre.shape[3:]
    cap = slots // devices
    feats, width = w_gate.shape[2:]
    tokens = route_ids.shape[1]
    experts = devices // GRP
    per_round = devices // 2 // ROUNDS
    rows = per_round * cap
    blocks = 2 * feats // LANES
    deep = -(-blocks * cap // 16) * 16
    vmem = pl.BlockSpec(memory_space=pltpu.VMEM)
    hbm = pl.BlockSpec(memory_space=pl.ANY)
    bf16 = jnp.bfloat16
    dma = pltpu.SemaphoreType.DMA
    out = pl.pallas_call(
        functools.partial(kernel, sections, devices, cap),
        out_shape=jax.ShapeDtypeStruct((tokens, GRP * feats), bf16),
        in_specs=[vmem, vmem, vmem, vmem, hbm, hbm],
        out_specs=vmem,
        scratch_shapes=[
            pltpu.VMEM((CHIPS, ROUNDS, 2, rows, 2 * hidden), bf16),
            pltpu.VMEM((ROUNDS, rows, 2 * hidden), bf16),
            pltpu.VMEM((2, 2 * feats, width), bf16),
            pltpu.VMEM((rows, 2 * feats), jnp.float32),
            pltpu.VMEM((2, deep, LANES), jnp.float32),
            pltpu.VMEM((ROUNDS, per_round, deep, LANES), bf16),
            pltpu.VMEM((CHIPS, experts, deep, LANES), bf16),
            pltpu.VMEM((1, tokens), jnp.int32),
            pltpu.VMEM((blocks * tokens, experts * deep), bf16),
            dma((CHIPS, ROUNDS, 2)),
            dma((ROUNDS, 5)),
            dma((ROUNDS, 4)),
            dma((2,)),
            dma((2,)),
            dma((2,)),
            dma((1,)),
            dma((1,)),
            dma((ROUNDS, per_round)),
            dma((CHIPS, experts)),
        ],
        compiler_params=pltpu.CompilerParams(
            collective_id=0, has_side_effects=True, vmem_limit_bytes=48 * 1024 * 1024
        ),
        name="moe_input_grad",
    )(
        route_ids.reshape(1, tokens),
        gate_pre[0, 0, 0],
        up_pre[0, 0, 0],
        hid_grad[0, 0, 0],
        w_gate[0, 0],
        w_up[0, 0],
    )
    return out[None]


def solution(mesh):
    placed = (
        P(None, ("section", "expert"), None),
        P("section", None, "expert", None, None),
        P("section", None, "expert", None, None),
        P("section", None, "expert", None, None),
        P("section", "expert", None, None),
        P("section", "expert", None, None),
    )
    return jax.shard_map(
        local,
        mesh=mesh,
        in_specs=placed,
        out_specs=P(None, ("section", "expert"), None),
        check_vma=False,
    )
```

time: 249 us -> 101 us (0.41)
  waiting for transfers between devices: 181 us -> 0 us
  Pallas kernels: 0 us -> 93.6 us
  starting transfers between devices: 25.7 us -> 0 us
  local copies, waits for them, and re-layouts: 23.9 us -> 6.82 us
  other arithmetic: 14.9 us -> 0 us
  matrix products: 2.8 us -> 0 us
    ppermute x4 -> x0, waiting for transfers between devices: 153 us -> none  [the longest x3 131 us: partner_2(): lax.ppermute(x, axis, [(i, i ^ 1 << apart) for i in range(lax.axis_size(a...]
    pallas_call x0 -> x1, Pallas kernels: none -> 93.6 us  [local(): pl.pallas_call(functools.partial(kernel, sections, devices, cap), out_sha...]
    all_to_all x1 -> x0, waiting for transfers between devices: 28.1 us -> none  [local(): lax.all_to_all(rows_out[None], 'expert', split_axis=1, concat_axis=1, til...]
    ppermute x4 -> x0, starting transfers between devices: 21.2 us -> none  [the longest x3 19.9 us: partner_2(): lax.ppermute(x, axis, [(i, i ^ 1 << apart) for i in range(lax.axis_size(a...]
    unnamed x1 -> x0, other arithmetic: 7.64 us -> none
    all_to_all x1 -> x0, local copies, waits for them, and re-layouts: 6.98 us -> none  [local(): lax.all_to_all(rows_out[None], 'expert', split_axis=1, concat_axis=1, til...]
    broadcast_in_dim x1 -> x0, local copies, waits for them, and re-layouts: 5.78 us -> none  [local(): rows_out[None]]
    select_n x3 -> x0, other arithmetic: 5.34 us -> none  [collect_group(): jnp.where(lower, jnp.concatenate([pieces, partner], 1), jnp.concatenate([...]
  transfers between devices with their start and end apart: 5 -> 0, of which waited for: 5 -> 0; matrix products, arithmetic and copies ran while one was open for 1% -> 0% of each run, Pallas kernels for 0% -> 0%
where the time goes in v1:
time: 101 us; the launch traced here: 100 us
  Pallas kernels  93.6 us (93%)
  local copies, waits for them, and re-layouts  6.82 us (7%)
    pallas_call x1, Pallas kernels, local(): pl.pallas_call(functools.partial(kernel, sections, devices, cap), out_sha...  93.6 us
    unnamed x13, local copies, waits for them, and re-layouts  6.82 us

profile of v1, /device:TPU:1, one launch (start us, length us, event | category | flops | bytes accessed | tf_op | source)
XLA Modules:
  0.0 100.4 jit_solution(16543099151501885625)
XLA Ops:
  0.0 0.0 copy-start.5
  0.0 0.7 copy-done.5
  0.7 0.0 copy-start
  0.7 1.2 %copy-done = bf16[1,1,448,1024]{3,2,1,0:T(8,128)(2,1)S(1)} copy-done((bf16[1,1,448,1024]{3,2,1,0:T(8,128)(2,1)S(1)}, bf16[1,1,448,1024]{3,2,1,0:T(8,128)(2,1)}, u32[]{:S(2)}) %copy-start) | copy-done | bytes 917528
  1.8 0.0 copy-start.1
  1.8 1.2 %copy-done.1 = bf16[1,1,448,1024]{3,2,1,0:T(8,128)(2,1)S(1)} copy-done((bf16[1,1,448,1024]{3,2,1,0:T(8,128)(2,1)S(1)}, bf16[1,1,448,1024]{3,2,1,0:T(8,128)(2,1)}, u32[]{:S(2)}) %copy-start.1) | copy-done | bytes 917528
  3.0 0.0 copy-start.2
  3.0 1.0 copy-done.2
  4.0 0.0 copy-start.3
  4.0 1.0 copy-done.3
  4.9 0.0 copy-start.4
  4.9 1.0 copy-done.4
  5.9 93.6 %moe_input_grad.1 = bf16[128,3584]{1,0:T(8,128)(2,1)S(1)} custom-call(s32[1,128]{1,0:T(1,128)S(1)} %bitcast.13, bf16[1152,128]{1,0:T(8,128)(2,1)S(1)} %bitcast.10, bf16[1152,128]{1,0:T(8,128)(2,1)S(1)} %bitcast.11, bf16[1152,128]{1,0:T(8,128)(2,1)S(1)} %bitcast.12, bf16[448,1024]{1,0:T(8,128)(2,1)S(1)} %bitcast.8, bf16[448,1024]{1,0:T(8,128)(2,1)S(1)} %bitcast.9), custom_call_target="tpu_custom_call" | custom-call | tf_op jit(solution)/shard_map/moe_input_grad/pallas_call | solution.py:348
  99.5 0.9 copy.8
Async XLA Ops:
  0.0 0.7 copy-start.5
  0.7 1.2 %copy-start = (bf16[1,1,448,1024]{3,2,1,0:T(8,128)(2,1)S(1)}, bf16[1,1,448,1024]{3,2,1,0:T(8,128)(2,1)}, u32[]{:S(2)}) copy-start(bf16[1,1,448,1024]{3,2,1,0:T(8,128)(2,1)} %param.10) | copy-start | bytes 2752516
  1.8 1.2 %copy-start.1 = (bf16[1,1,448,1024]{3,2,1,0:T(8,128)(2,1)S(1)}, bf16[1,1,448,1024]{3,2,1,0:T(8,128)(2,1)}, u32[]{:S(2)}) copy-start(bf16[1,1,448,1024]{3,2,1,0:T(8,128)(2,1)} %param.11) | copy-start | bytes 2752516
  3.0 1.0 copy-start.2
  4.0 1.0 copy-start.3
  4.9 1.0 copy-start.4

commit v2 on v1

--- a/solution.py
+++ b/solution.py
@@ -10,6 +10,8 @@
 GRP = 8
 CHIPS = 4
 ROUNDS = 4
+GRID_X, GRID_Y = 4, 8
+SPREAD = GRID_X // 2 + GRID_Y // 2 + 1
 LANES = 128
 MESH = pl.DeviceIdType.MESH
 
@@ -18,8 +20,8 @@
     sections, devices, cap,
     ids_ref, gate_ref, up_ref, hid_ref, wg_ref, wu_ref,
     out_ref,
-    act, other, weight, acc, stage, msg, recv, ids_in, pick,
-    act_recv, own_send, fwd_send, w_send, w_recv, w_local, id_send, id_recv, msg_send, msg_recv,
+    gate_in, up_in, hid_in, act, other, weight, acc, stage, msg, recv, ids_in, pick,
+    act_recv, own_send, fwd_send, w_send, w_recv, w_local, in_local, id_send, id_recv, msg_send, msg_recv, told,
 ):
     experts = devices // GRP
     half = devices // 2
@@ -41,52 +43,66 @@
 
     has_left, has_right = c > 0, c < CHIPS - 1
     sends_back, gets_back = s > 0, s < sections - 1
+    x, y = p // (2 * GRID_Y), p // 2 % GRID_Y
+
+    def at_grid(gx, gy):
+        return (s, ((gx + GRID_X) % GRID_X * GRID_Y + (gy + GRID_Y) % GRID_Y) * 2 + k)
 
     barrier = pltpu.get_barrier_semaphore()
 
     def greet(device):
         pl.semaphore_signal(barrier, inc=1, device_id=device, device_id_type=MESH)
 
-    greet(near(c, 1 - k))
-
-    @pl.when(has_left)
-    def _():
-        greet(near(c - 1, 0))
-        greet(near(c - 1, 1))
-
-    @pl.when(has_right)
-    def _():
-        greet(near(c + 1, 0))
-        greet(near(c + 1, 1))
-
     @pl.when(gets_back)
     def _():
         greet((s + 1, p))
-        owner_half = p // half
-
-        def step(i, carry):
-            greet((s + 1, 2 * i + owner_half))
-            return carry
-
-        lax.fori_loop(0, devices // 2, step, 0)
+
+    @pl.when(sends_back)
+    def _():
+        greet(near(c, 1 - k))
+        for gx, gy in ((x - 1, y), (x + 1, y), (x, y - 1), (x, y + 1)):
+            greet(at_grid(gx, gy))
+
+        @pl.when(has_left)
+        def _():
+            greet(near(c - 1, 1 - k))
+
+        @pl.when(has_right)
+        def _():
+            greet(near(c + 1, 1 - k))
+
+    def tell(step):
+        if step < GRID_X // 2:
+            devices_told = [at_grid(x - 1, y), at_grid(x + 1, y)]
+        elif step < SPREAD - 1:
+            devices_told = [at_grid(x, y - 1), at_grid(x, y + 1)]
+        else:
+            devices_told = [near(c, 1 - k)]
+        for device in devices_told:
+            pl.semaphore_signal(told.at[step], inc=1, device_id=device, device_id_type=MESH)
+
+    def hear(step):
+        pl.semaphore_wait(told.at[step], 1 if step == SPREAD - 1 else 2)
 
     w_rows = pl.ds(pl.multiple_of(k * feats, feats), feats)
     local_g = pltpu.make_async_copy(wg_ref, weight.at[0, w_rows], w_local.at[0])
     local_u = pltpu.make_async_copy(wu_ref, weight.at[1, w_rows], w_local.at[1])
-    local_g.start()
-    local_u.start()
+    loads = [
+        pltpu.make_async_copy(ref, dst, in_local.at[i])
+        for i, (ref, dst) in enumerate(((gate_ref, gate_in), (up_ref, up_in), (hid_ref, hid_in)))
+    ]
 
     def derive(start):
         at = pl.ds(pl.multiple_of(start, 16), rows)
-        gate_val = gate_ref[at, :].astype(jnp.float32)
-        up_val = up_ref[at, :].astype(jnp.float32)
-        grad_val = hid_ref[at, :].astype(jnp.float32)
+        gate_val = gate_in[at, :].astype(jnp.float32)
+        up_val = up_in[at, :].astype(jnp.float32)
+        grad_val = hid_in[at, :].astype(jnp.float32)
         sigma = jax.nn.sigmoid(gate_val)
         part = grad_val * sigma
         gate_grad = part * up_val * (1.0 + gate_val * (1.0 - sigma))
         return gate_grad.astype(jnp.bfloat16), (part * gate_val).astype(jnp.bfloat16)
 
-    def derive_round(r, carry):
+    def derive_round(r):
         chunk = (r + turn) % ROUNDS
         gate_grad, up_grad = derive(k * half_rows + chunk * rows)
         act[c, r, k, :, :LANES] = gate_grad
@@ -94,17 +110,6 @@
         gate_grad, up_grad = derive((1 - k) * half_rows + chunk * rows)
         other[r, :, :LANES] = gate_grad
         other[r, :, LANES:] = up_grad
-        return carry
-
-    lax.fori_loop(0, ROUNDS, derive_round, 0)
-
-    pl.semaphore_wait(
-        barrier,
-        1
-        + 2 * has_left.astype(jnp.int32)
-        + 2 * has_right.astype(jnp.int32)
-        + (devices // 2 + 1) * sends_back.astype(jnp.int32),
-    )
 
     def remote(src, dst, send, recv_sem, device):
         return pltpu.make_async_remote_copy(
@@ -151,15 +156,35 @@
     weight_u = remote(wu_ref, weight.at[1, w_rows], w_send.at[1], w_recv.at[1], near(c, 1 - k))
     id_copy = remote(ids_ref, ids_in, id_send.at[0], id_recv.at[0], (s - 1, p))
 
-    each_own(0, lambda copy: copy.start())
-    weight_g.start()
-    weight_u.start()
-
     @pl.when(sends_back)
     def _():
+        for load in loads:
+            load.start()
+        local_g.start()
+        local_u.start()
+        for load in loads:
+            load.wait()
+        derive_round(0)
+        pl.semaphore_wait(
+            barrier, 6 + has_left.astype(jnp.int32) + has_right.astype(jnp.int32)
+        )
+        each_own(0, lambda copy: copy.start())
+        weight_g.start()
+        weight_u.start()
         id_copy.start()
-
-    stage[...] = jnp.zeros_like(stage)
+        tell(0)
+
+        def early(r, carry):
+            derive_round(r)
+
+            @pl.when(r == 1)
+            def _():
+                each_own(1, lambda copy: copy.start())
+
+            return carry
+
+        lax.fori_loop(1, ROUNDS, early, 0)
+        stage[...] = jnp.zeros_like(stage)
 
     def back(r, i):
         owner = k * half + ((r + turn) % ROUNDS) * per_round + i
@@ -167,8 +192,8 @@
             msg.at[r, i], recv.at[c, e], msg_send.at[r, i], msg_recv.at[c, e], (s - 1, owner)
         )
 
-    def round_step(r, carry):
-        @pl.when(r + 1 < ROUNDS)
+    def relay(r):
+        @pl.when((r > 0) & (r + 1 < ROUNDS))
         def _():
             each_own(r + 1, lambda copy: copy.start())
 
@@ -190,6 +215,12 @@
             def _():
                 forward(r, c + 1, c - 1, 1).start()
 
+        for turn_of in range(2):
+            @pl.when(r == turn_of)
+            def _(step=2 * turn_of):
+                hear(step)
+                tell(step + 1)
+
         @pl.when(c >= 2)
         def _():
             arrived(act.at[c - 2, r], act_recv.at[c - 2, r, 0])
@@ -206,6 +237,13 @@
             def _():
                 forward(r, c + 2, c - 1, 3).start()
 
+        for turn_of in range(2):
+            @pl.when(r == turn_of)
+            def _(step=2 * turn_of + 1):
+                hear(step)
+                tell(step + 1)
+
+    def compute(r):
         arrived(act.at[c, r, 1 - k], act_recv.at[c, r, 1 - k])
 
         @pl.when(r == 0)
@@ -223,6 +261,11 @@
         @pl.when(c == 0)
         def _():
             arrived(act.at[CHIPS - 1, r], act_recv.at[CHIPS - 1, r, 0])
+
+        @pl.when(r == 0)
+        def _():
+            hear(4)
+            tell(5)
 
         lhs = [
             jnp.concatenate(
@@ -242,22 +285,40 @@
                 total = term if total is None else total + term
             acc[:, start:start + size] = total
 
+        @pl.when(r == 0)
+        def _():
+            hear(5)
+            tell(6)
+
         for i in range(per_round):
             for n in range(blocks):
                 stage[i % 2, n * cap:(n + 1) * cap, :] = acc[i * cap:(i + 1) * cap, n * LANES:(n + 1) * LANES]
             msg[r, i] = stage[i % 2].astype(jnp.bfloat16)
 
-        @pl.when(sends_back)
-        def _():
-            def send(i, carry):
-                back(r, (i + 2 * c + e) % per_round).start()
-                return carry
-
-            lax.fori_loop(0, per_round, send, 0)
+        @pl.when(r == 0)
+        def _():
+            hear(6)
+
+        def send(i, carry):
+            back(r, (i + 2 * c + e) % per_round).start()
+            return carry
+
+        lax.fori_loop(0, per_round, send, 0)
+
+    def round_step(r, carry):
+        @pl.when(r < ROUNDS)
+        def _():
+            relay(r)
+
+        @pl.when(r > 0)
+        def _():
+            compute(r - 1)
 
         return carry
 
-    lax.fori_loop(0, ROUNDS, round_step, 0)
+    @pl.when(sends_back)
+    def _():
+        lax.fori_loop(0, ROUNDS + 1, round_step, 0)
 
     deep = recv.shape[2]
     width = experts * deep
@@ -294,13 +355,6 @@
     def _():
         out_ref[...] = jnp.zeros_like(out_ref)
 
-    weight_g.wait_send()
-    weight_u.wait_send()
-
-    @pl.when(sends_back)
-    def _():
-        id_copy.wait_send()
-
     def drain(r, carry):
         each_own(r, lambda copy: copy.wait_send())
 
@@ -317,17 +371,19 @@
         def _():
             forward(r, c + 2, c - 1, 3).wait_send()
 
-        @pl.when(sends_back)
-        def _():
-            def done(i, carry):
-                back(r, i).wait_send()
-                return carry
-
-            lax.fori_loop(0, per_round, done, 0)
-
+        def done(i, carry):
+            back(r, i).wait_send()
+            return carry
+
+        lax.fori_loop(0, per_round, done, 0)
         return carry
 
-    lax.fori_loop(0, ROUNDS, drain, 0)
+    @pl.when(sends_back)
+    def _():
+        weight_g.wait_send()
+        weight_u.wait_send()
+        id_copy.wait_send()
+        lax.fori_loop(0, ROUNDS, drain, 0)
 
 
 def local(route_ids, gate_pre, up_pre, hid_grad, w_gate, w_up):
@@ -348,9 +404,12 @@
     out = pl.pallas_call(
         functools.partial(kernel, sections, devices, cap),
         out_shape=jax.ShapeDtypeStruct((tokens, GRP * feats), bf16),
-        in_specs=[vmem, vmem, vmem, vmem, hbm, hbm],
+        in_specs=[vmem, hbm, hbm, hbm, hbm, hbm],
         out_specs=vmem,
         scratch_shapes=[
+            pltpu.VMEM((slots, hidden), bf16),
+            pltpu.VMEM((slots, hidden), bf16),
+            pltpu.VMEM((slots, hidden), bf16),
             pltpu.VMEM((CHIPS, ROUNDS, 2, rows, 2 * hidden), bf16),
             pltpu.VMEM((ROUNDS, rows, 2 * hidden), bf16),
             pltpu.VMEM((2, 2 * feats, width), bf16),
@@ -366,13 +425,15 @@
             dma((2,)),
             dma((2,)),
             dma((2,)),
+            dma((3,)),
             dma((1,)),
             dma((1,)),
             dma((ROUNDS, per_round)),
             dma((CHIPS, experts)),
+            pltpu.SemaphoreType.REGULAR((SPREAD,)),
         ],
         compiler_params=pltpu.CompilerParams(
-            collective_id=0, has_side_effects=True, vmem_limit_bytes=48 * 1024 * 1024
+            collective_id=0, has_side_effects=True, vmem_limit_bytes=67_043_328
         ),
         name="moe_input_grad",
     )(

time: 101 us -> 97.6 us (0.966)
  the two profiles are of different devices: /device:TPU:1 before, /device:TPU:4 now
where the time goes in v2:
time: 97.6 us; the launch traced here: 97.4 us
  Pallas kernels  95.3 us (98%)
  local copies, waits for them, and re-layouts  2.16 us (2%)
    pallas_call x1, Pallas kernels, local(): pl.pallas_call(functools.partial(kernel, sections, devices, cap), out_sha...  95.3 us
    unnamed x1, local copies, waits for them, and re-layouts  2.16 us

profile of v2, /device:TPU:4, one launch (start us, length us, event | category | flops | bytes accessed | tf_op | source)
XLA Modules:
  0.0 97.4 jit_solution(13750650134234514634)
XLA Ops:
  0.0 95.3 %moe_input_grad.1 = bf16[128,3584]{1,0:T(8,128)(2,1)} custom-call(s32[1,128]{1,0:T(1,128)} %bitcast.13, bf16[1152,128]{1,0:T(8,128)(2,1)} %bitcast.10, bf16[1152,128]{1,0:T(8,128)(2,1)} %bitcast.11, bf16[1152,128]{1,0:T(8,128)(2,1)} %bitcast.12, bf16[448,1024]{1,0:T(8,128)(2,1)} %bitcast.8, bf16[448,1024]{1,0:T(8,128)(2,1)} %bitcast.9), custom_call_target="tpu_custom_call" | custom-call | tf_op jit(solution)/shard_map/moe_input_grad/pallas_call | solution.py:404
  95.3 2.2 %copy.8 = bf16[1,128,3584]{2,1,0:T(8,128)(2,1)} copy(bf16[1,128,3584]{2,1,0:T(8,128)(2,1)} %bitcast.7) | data formatting | bytes 1835008

commit v3 on v2

--- a/solution.py
+++ b/solution.py
@@ -10,6 +10,7 @@
 GRP = 8
 CHIPS = 4
 ROUNDS = 4
+AHEAD = 4
 GRID_X, GRID_Y = 4, 8
 SPREAD = GRID_X // 2 + GRID_Y // 2 + 1
 LANES = 128
@@ -93,7 +94,7 @@
     ]
 
     def derive(start):
-        at = pl.ds(pl.multiple_of(start, 16), rows)
+        at = pl.ds(pl.multiple_of(start, 8), rows)
         gate_val = gate_in[at, :].astype(jnp.float32)
         up_val = up_in[at, :].astype(jnp.float32)
         grad_val = hid_in[at, :].astype(jnp.float32)
@@ -177,9 +178,9 @@
         def early(r, carry):
             derive_round(r)
 
-            @pl.when(r == 1)
+            @pl.when(r < AHEAD)
             def _():
-                each_own(1, lambda copy: copy.start())
+                each_own(r, lambda copy: copy.start())
 
             return carry
 
@@ -193,9 +194,9 @@
         )
 
     def relay(r):
-        @pl.when((r > 0) & (r + 1 < ROUNDS))
-        def _():
-            each_own(r + 1, lambda copy: copy.start())
+        @pl.when((r > 0) & (r + AHEAD - 1 < ROUNDS))
+        def _():
+            each_own(r + AHEAD - 1, lambda copy: copy.start())
 
         @pl.when(has_left)
         def _():
@@ -305,20 +306,18 @@
 
         lax.fori_loop(0, per_round, send, 0)
 
-    def round_step(r, carry):
-        @pl.when(r < ROUNDS)
-        def _():
+    @pl.when(sends_back)
+    def _():
+        def relay_step(r, carry):
             relay(r)
-
-        @pl.when(r > 0)
-        def _():
-            compute(r - 1)
-
-        return carry
-
-    @pl.when(sends_back)
-    def _():
-        lax.fori_loop(0, ROUNDS + 1, round_step, 0)
+            return carry
+
+        def compute_step(r, carry):
+            compute(r)
+            return carry
+
+        lax.fori_loop(0, ROUNDS, relay_step, 0)
+        lax.fori_loop(0, ROUNDS, compute_step, 0)
 
     deep = recv.shape[2]
     width = experts * deep
@@ -337,11 +336,11 @@
         for n in range(blocks):
             pick[n * tokens:(n + 1) * tokens, :] = jnp.where(lane == n * cap, 1.0, 0.0).astype(jnp.bfloat16)
 
-        for chip in range(CHIPS):
-            for expert_at in range(experts):
-                arrived(recv.at[chip, expert_at], msg_recv.at[chip, expert_at])
-
         for pair in range(0, CHIPS, 2):
+            for chip in (pair, pair + 1):
+                for expert_at in range(experts):
+                    arrived(recv.at[chip, expert_at], msg_recv.at[chip, expert_at])
+
             rhs = jnp.concatenate(
                 [recv[pair].reshape(width, LANES), recv[pair + 1].reshape(width, LANES)], axis=1
             )

time: 97.6 us -> 94.4 us (0.967)
  the two profiles are of different devices: /device:TPU:4 before, /device:TPU:391 now
where the time goes in v3:
time: 94.4 us; the launch traced here: 94.2 us
  Pallas kernels  92.1 us (98%)
  local copies, waits for them, and re-layouts  2.16 us (2%)
    pallas_call x1, Pallas kernels, local(): pl.pallas_call(functools.partial(kernel, sections, devices, cap), out_sha...  92.1 us
    unnamed x1, local copies, waits for them, and re-layouts  2.16 us

profile of v3, /device:TPU:391, one launch (start us, length us, event | category | flops | bytes accessed | tf_op | source)
XLA Modules:
  0.0 94.2 jit_solution(10797616097381338277)
XLA Ops:
  0.0 92.1 %moe_input_grad.1 = bf16[128,3584]{1,0:T(8,128)(2,1)} custom-call(s32[1,128]{1,0:T(1,128)} %bitcast.13, bf16[1152,128]{1,0:T(8,128)(2,1)} %bitcast.10, bf16[1152,128]{1,0:T(8,128)(2,1)} %bitcast.11, bf16[1152,128]{1,0:T(8,128)(2,1)} %bitcast.12, bf16[448,1024]{1,0:T(8,128)(2,1)} %bitcast.8, bf16[448,1024]{1,0:T(8,128)(2,1)} %bitcast.9), custom_call_target="tpu_custom_call" | custom-call | tf_op jit(solution)/shard_map/moe_input_grad/pallas_call | solution.py:403
  92.1 2.2 %copy.8 = bf16[1,128,3584]{2,1,0:T(8,128)(2,1)} copy(bf16[1,128,3584]{2,1,0:T(8,128)(2,1)} %bitcast.7) | data formatting | bytes 1835008

commit v4 on v3

--- a/solution.py
+++ b/solution.py
@@ -37,7 +37,7 @@
     e = p // GRP
     c = (p % GRP) // 2
     k = p % 2
-    turn = e % ROUNDS
+    turn = (e + 1) % ROUNDS
 
     def near(chip, core):
         return (s, e * GRP + chip * 2 + core)

time: 94.4 us -> 92.4 us (0.979)
  the two profiles are of different devices: /device:TPU:391 before, /device:TPU:1 now
where the time goes in v4:
time: 92.4 us; the launch traced here: 90.6 us
  Pallas kernels  88.4 us (96%)
  local copies, waits for them, and re-layouts  2.16 us (2%)
    pallas_call x1, Pallas kernels, local(): pl.pallas_call(functools.partial(kernel, sections, devices, cap), out_sha...  88.4 us
    unnamed x1, local copies, waits for them, and re-layouts  2.16 us

profile of v4, /device:TPU:1, one launch (start us, length us, event | category | flops | bytes accessed | tf_op | source)
XLA Modules:
  0.0 90.6 jit_solution(507224089341129720)
XLA Ops:
  0.0 88.4 %moe_input_grad.1 = bf16[128,3584]{1,0:T(8,128)(2,1)} custom-call(s32[1,128]{1,0:T(1,128)} %bitcast.13, bf16[1152,128]{1,0:T(8,128)(2,1)} %bitcast.10, bf16[1152,128]{1,0:T(8,128)(2,1)} %bitcast.11, bf16[1152,128]{1,0:T(8,128)(2,1)} %bitcast.12, bf16[448,1024]{1,0:T(8,128)(2,1)} %bitcast.8, bf16[448,1024]{1,0:T(8,128)(2,1)} %bitcast.9), custom_call_target="tpu_custom_call" | custom-call | tf_op jit(solution)/shard_map/moe_input_grad/pallas_call | solution.py:403
  88.4 2.2 %copy.8 = bf16[1,128,3584]{2,1,0:T(8,128)(2,1)} copy(bf16[1,128,3584]{2,1,0:T(8,128)(2,1)} %bitcast.7) | data formatting | bytes 1835008
